TPU v7x, 512 devices: a whole 4x4x16 slice. The times are simulated.
512 devices in a mesh: slab: 64 (over z, x), sec: 8 (over y, core).
Axes of the slice: x: 4, y: 4, z: 16, core: 2. Of those that a mesh axis runs over, the one named last changes fastest.
Arguments:
- source: float32 [64, 65536], P(None, ('slab', 'sec'))
- fine_blocks: bfloat16 [3, 64, 64, 65536], P(None, None, None, ('slab', 'sec'))
- fine_pattern: int32 [3, 65536], P(None, ('slab', 'sec')), may hold values from 0 to 65535, as said below
- fine_prolong: bfloat16 [3, 64, 6, 65536], P(None, None, None, ('slab', 'sec')), may hold values from -0.75 to 0.75
- prolong_pattern: int32 [3, 65536], P(None, ('slab', 'sec')), may hold values from 0 to 65535, as said below
- coarse_blocks: bfloat16 [3, 6, 6, 65536], P(None, None, None, 'slab')
- coarse_pattern: int32 [3, 65536], P(None, 'slab'), may hold values from 0 to 65535, as said below
- section_prolong: bfloat16 [3, 6, 24, 65536], P(None, None, None, 'slab'), may hold values from -0.046875 to 0.046875
- coarsest_inverse: float32 [1536, 1536], P('slab')
Outputs:
- solution: float32 [64, 65536], P(None, ('slab', 'sec'))
Inputs may be any that keep to these rules, and one draw needn't show every extreme that they name: `fine_pattern`: row 0 names the aggregate itself; the other rows name aggregates at most 96 away, and distance exactly 96 occurs in every draw. `prolong_pattern`: row 0 names the aggregate's own coarse block; the other rows name coarse blocks at most 96 away, and distance exactly 96 occurs in every draw. `coarse_pattern`: row 0 names the block itself; the other rows name coarse blocks at most 96 away, and distance exactly 96 occurs in every draw.
All inputs are finite; a program needn't handle non-finite values.
Results may differ from a plain program's by a relative error of at most 0.0003.
Values sent between devices are 32-bit elements; how exact they have to be, the bound alone decides.
No kernel may reach another device: no remote copies, remote signals or barrier semaphores. Data moves between devices by JAX's collectives and lax.ppermute only.
A program may use at most 64 MiB of HBM per device.

v0:
```python
import jax
import jax.numpy as jnp
from jax import lax
from jax.sharding import PartitionSpec as P

HB = 96
CYCLES = 2
KEEP = 1.0 / 7.0
FRESH = 8.0 / 7.0


def padded(array, sides, width):
    for axis, dim in sides:
        count, length = (lax.axis_size(axis), array.shape[dim])
        up = [(i, (i + 1) % count) for i in range(count - 1)]
        down = [(j, i) for i, j in up]
        last = lax.slice_in_dim(array, length - width, length, axis=dim)
        leading = lax.slice_in_dim(array, 0, width, axis=dim)
        before = lax.ppermute(last, axis, up)
        after = lax.ppermute(leading, axis, down)
        array = jnp.concatenate([before, array, after], axis=dim)
    return array


def from_behind(value, axis, steps):
    count = lax.axis_size(axis)
    leading, last = (max(0, -steps), min(count, count - steps))
    return lax.ppermute(value, axis, [(source, source + steps) for source in range(leading, last)])


def inverse_diagonal(matrix):
    return 1.0 / jnp.diagonal(matrix[0], axis1=0, axis2=1).T.astype(jnp.float32)


def apply_local(matrix, local_cols, extended):
    picked = jnp.swapaxes(extended[:, local_cols], 0, 1)
    return jnp.sum(matrix * picked[:, None, :, :], axis=(0, 2))


def smooth(operator, inverse, rhs, start):
    if start is None:
        change = inverse * rhs
        field = change
    else:
        change = inverse * (rhs - operator(start))
        field = start + change
    change = KEEP * change + FRESH * inverse * (rhs - operator(field))
    return field + change


def shards(
    source,
    fine_blocks,
    fine_pattern,
    fine_prolong,
    prolong_pattern,
    coarse_blocks,
    coarse_pattern,
    section_prolong,
    coarsest_inverse,
):
    reach = HB
    own_rows = source.shape[1]
    section_rows = coarse_blocks.shape[3]
    device = lax.axis_index(("slab", "sec"))
    section = lax.axis_index("slab")
    fine_cols = fine_pattern - (device * own_rows - reach)
    coarse_cols = coarse_pattern - (section * section_rows - reach)
    gather_cols = prolong_pattern - (section * section_rows - reach)
    fine_inverse = inverse_diagonal(fine_blocks)
    coarse_inverse = inverse_diagonal(coarse_blocks)

    def fine_apply(field):
        extended = padded(field, ((("slab", "sec"), 1),), reach)
        return apply_local(fine_blocks, fine_cols, extended)

    def coarse_extend(field):
        return padded(field, (("slab", 1),), reach)

    def coarse_apply(field):
        return apply_local(coarse_blocks, coarse_cols, coarse_extend(field))

    solution = None
    for turn_index in range(CYCLES):
        solution = smooth(fine_apply, fine_inverse, source, solution)
        residual = source - fine_apply(solution)
        terms = jnp.sum(fine_prolong * residual[None, :, None, :], axis=1)
        modes = terms.shape[1]
        flat = jnp.swapaxes(terms, 0, 1).reshape(modes, -1)
        slots = gather_cols.reshape(-1)
        partial_sum = (
            jnp.zeros((modes, section_rows + 2 * reach), jnp.float32).at[:, slots].add(flat)
        )
        partial_sum = lax.psum(partial_sum, "sec")
        lower = from_behind(partial_sum[:, section_rows + reach :], "slab", 1)
        upper = from_behind(partial_sum[:, :reach], "slab", -1)
        inner = partial_sum[:, reach : reach + section_rows]
        coarse_rhs = inner.at[:, :reach].add(lower).at[:, section_rows - reach :].add(upper)
        coarse_sol = smooth(coarse_apply, coarse_inverse, coarse_rhs, None)
        coarse_res = coarse_rhs - coarse_apply(coarse_sol)
        parts = jnp.sum(section_prolong * coarse_res[None, :, None, :], axis=(1, 3))
        width = parts.shape[1]
        every = lax.all_gather(parts[None], "slab", axis=0, tiled=True)
        zero = jnp.zeros((1, width), jnp.float32)
        total = (
            every[:, 1]
            + jnp.concatenate([every[1:, 0], zero], 0)
            + jnp.concatenate([zero, every[:-1, 2]], 0)
        )
        answer = jnp.dot(coarsest_inverse, total.reshape(-1), precision=lax.Precision.HIGHEST)
        nearby = padded(answer[None, :], (("slab", 0),), 1)
        coarse_sol = coarse_sol + jnp.sum(section_prolong * nearby[:, None, :, None], axis=(0, 2))
        coarse_sol = smooth(coarse_apply, coarse_inverse, coarse_rhs, coarse_sol)
        prolong_extended = coarse_extend(coarse_sol)
        picked = jnp.swapaxes(prolong_extended[:, gather_cols], 0, 1)
        solution = solution + jnp.sum(fine_prolong * picked[:, None, :, :], axis=(0, 2))
        solution = smooth(fine_apply, fine_inverse, source, solution)
    return solution


def solution(mesh):
    in_specs = (
        P(None, ("slab", "sec")),
        P(None, None, None, ("slab", "sec")),
        P(None, ("slab", "sec")),
        P(None, None, None, ("slab", "sec")),
        P(None, ("slab", "sec")),
        P(None, None, None, "slab"),
        P(None, "slab"),
        P(None, None, None, "slab"),
        P("slab", None),
    )
    out_specs = P(None, ("slab", "sec"))
    return jax.shard_map(shards, mesh=mesh, in_specs=in_specs, out_specs=out_specs, check_vma=False)
```

profile of v0, /device:TPU:127, one launch (start us, length us, event | category | flops | bytes accessed | tf_op | source)
XLA Modules:
  0.0 759.0 jit_solution(1430777949323937785)
XLA Ops:
  4.9 4.9 collective-permute-start
  16.5 3.9 collective-permute-done.1
  25.9 5.1 collective-permute-start.2
  33.6 8.1 %collective-permute-done.3 = f32[64,96]{1,0:T(8,128)S(1)} collective-permute-done((f32[64,96]{1,0:T(8,128)S(1)}, f32[64,96]{1,0:T(8,128)S(1)}, u32[]{:S(2)}, u32[]{:S(2)}) %collective-permute-start.3) | collective-permute-done | bytes 24608 | tf_op jit(solution)/shard_map/ppermute | solution.py:20
  53.9 23.9 %psum.14 = f32[6,1216]{1,0:T(8,128)S(1)} all-reduce(f32[6,1216]{1,0:T(8,128)S(1)} %copy.153), channel_id=1, replica_groups=mesh['slab'=64,'sec'=8] {'sec'}, use_global_device_ids=true, to_apply=%region_4.5 | all-reduce | flops 7296 | bytes 58368 | tf_op jit(solution)/shard_map/psum | solution.py:94
  86.0 3.4 collective-permute-done.5
  91.7 3.4 collective-permute-start.7
  95.8 3.6 collective-permute-done.7
  100.5 11.9 %gather_fusion.4 = f32[3072,6]{1,0:T(8,128)} fusion(f32[6,1216]{0,1:T(8,128)} %copy.154, s32[3072]{0:T(1024)S(1)} %broadcast_clamp_fusion), kind=kCustom, calls=%fused_computation.4 | custom fusion | bytes 159744 | tf_op jit(solution)/shard_map/gather | solution.py:36
  117.4 3.4 collective-permute-start.9
  120.8 4.3 collective-permute-done.9
  126.3 11.9 %gather_fusion.5 = f32[3072,6]{1,0:T(8,128)} fusion(f32[6,1216]{0,1:T(8,128)} %copy.156, s32[3072]{0:T(1024)S(1)} %broadcast_clamp_fusion), kind=kCustom, calls=%fused_computation.5 | custom fusion | bytes 159744 | tf_op jit(solution)/shard_map/gather | solution.py:36
  142.6 72.8 %all-gather.2 = f32[64,3,24]{2,1,0:T(4,128)S(1)} all-gather(f32[1,3,24]{2,1,0:T(4,128)S(1)} %bitcast.134), channel_id=2, replica_groups=mesh['slab'=64,'sec'=8] {'slab'}, dimensions={0}, use_global_device_ids=true | all-gather | bytes 18720 | tf_op jit(solution)/shard_map/all_gather | solution.py:103
  216.3 4.2 collective-permute-start.10
  222.4 5.7 collective-permute-done.11
  231.5 3.4 collective-permute-start.13
  234.9 4.3 collective-permute-done.13
  240.4 11.9 %gather_fusion.6 = f32[3072,6]{1,0:T(8,128)} fusion(f32[6,1216]{0,1:T(8,128)} %copy.162, s32[3072]{0:T(1024)S(1)} %broadcast_clamp_fusion), kind=kCustom, calls=%fused_computation.6 | custom fusion | bytes 159744 | tf_op jit(solution)/shard_map/gather | solution.py:36
  257.9 3.4 collective-permute-start.15
  261.3 4.3 collective-permute-done.15
  268.2 11.9 %gather_fusion.7 = f32[3072,6]{1,0:T(8,128)} fusion(f32[6,1216]{0,1:T(8,128)} %copy.164, s32[3072]{0:T(1024)S(1)} %broadcast_clamp_fusion), kind=kCustom, calls=%fused_computation.7 | custom fusion | bytes 159744 | tf_op jit(solution)/shard_map/gather | solution.py:36
  285.7 3.4 collective-permute-start.17
  289.1 4.3 collective-permute-done.17
  299.4 38.0 %collective-permute-start.18 = (f32[64,96]{1,0:T(8,128)S(1)}, f32[64,96]{1,0:T(8,128)S(1)}, u32[]{:S(2)}, u32[]{:S(2)}) collective-permute-start(f32[64,96]{1,0:T(8,128)S(1)} %get-tuple-element.83), channel_id=1, source_target_pairs={{0,1},{1,2},{2,3},{3,4},{4,5},{5,6},{6,7},{7,8},{8,9},{9,10},{10,1... | collective-permute-start | bytes 73736 | tf_op jit(solution)/shard_map/ppermute | solution.py:19
  339.5 8.5 %collective-permute-done.19 = f32[64,96]{1,0:T(8,128)S(1)} collective-permute-done((f32[64,96]{1,0:T(8,128)S(1)}, f32[64,96]{1,0:T(8,128)S(1)}, u32[]{:S(2)}, u32[]{:S(2)}) %collective-permute-start.19) | collective-permute-done | bytes 24608 | tf_op jit(solution)/shard_map/ppermute | solution.py:20
  357.8 8.2 %collective-permute-done.21 = f32[64,96]{1,0:T(8,128)S(1)} collective-permute-done((f32[64,96]{1,0:T(8,128)S(1)}, f32[64,96]{1,0:T(8,128)S(1)}, u32[]{:S(2)}, u32[]{:S(2)}) %collective-permute-start.21) | collective-permute-done | bytes 24608 | tf_op jit(solution)/shard_map/ppermute | solution.py:20
  375.7 8.2 %collective-permute-done.23 = f32[64,96]{1,0:T(8,128)S(1)} collective-permute-done((f32[64,96]{1,0:T(8,128)S(1)}, f32[64,96]{1,0:T(8,128)S(1)}, u32[]{:S(2)}, u32[]{:S(2)}) %collective-permute-start.23) | collective-permute-done | bytes 24608 | tf_op jit(solution)/shard_map/ppermute | solution.py:20
  396.7 8.2 %collective-permute-done.25 = f32[64,96]{1,0:T(8,128)S(1)} collective-permute-done((f32[64,96]{1,0:T(8,128)S(1)}, f32[64,96]{1,0:T(8,128)S(1)}, u32[]{:S(2)}, u32[]{:S(2)}) %collective-permute-start.25) | collective-permute-done | bytes 24608 | tf_op jit(solution)/shard_map/ppermute | solution.py:20
  417.7 8.2 %collective-permute-done.27 = f32[64,96]{1,0:T(8,128)S(1)} collective-permute-done((f32[64,96]{1,0:T(8,128)S(1)}, f32[64,96]{1,0:T(8,128)S(1)}, u32[]{:S(2)}, u32[]{:S(2)}) %collective-permute-start.27) | collective-permute-done | bytes 24608 | tf_op jit(solution)/shard_map/ppermute | solution.py:20
  440.1 24.5 %psum.15 = f32[6,1216]{1,0:T(8,128)S(1)} all-reduce(f32[6,1216]{1,0:T(8,128)} %copy.179), channel_id=1, replica_groups=mesh['slab'=64,'sec'=8] {'sec'}, use_global_device_ids=true, to_apply=%region_20.21 | all-reduce | flops 7296 | bytes 58368 | tf_op jit(solution)/shard_map/psum | solution.py:94
  470.9 3.4 collective-permute-done.29
  476.6 3.4 collective-permute-start.31
  479.9 4.3 collective-permute-done.31
  485.4 11.9 %gather_fusion.14 = f32[3072,6]{1,0:T(8,128)} fusion(f32[6,1216]{0,1:T(8,128)} %copy.180, s32[3072]{0:T(1024)S(1)} %broadcast_clamp_fusion), kind=kCustom, calls=%fused_computation.14 | custom fusion | bytes 159744 | tf_op jit(solution)/shard_map/gather | solution.py:36
  502.9 3.4 collective-permute-start.33
  506.3 4.3 collective-permute-done.33
  511.8 11.9 %gather_fusion.15 = f32[3072,6]{1,0:T(8,128)} fusion(f32[6,1216]{0,1:T(8,128)} %copy.182, s32[3072]{0:T(1024)S(1)} %broadcast_clamp_fusion), kind=kCustom, calls=%fused_computation.15 | custom fusion | bytes 159744 | tf_op jit(solution)/shard_map/gather | solution.py:36
  528.8 70.7 %all-gather.3 = f32[64,3,24]{2,1,0:T(4,128)S(1)} all-gather(f32[1,3,24]{2,1,0:T(4,128)S(1)} %bitcast.135), channel_id=3, replica_groups=mesh['slab'=64,'sec'=8] {'slab'}, dimensions={0}, use_global_device_ids=true | all-gather | bytes 18720 | tf_op jit(solution)/shard_map/all_gather | solution.py:103
  603.5 4.2 collective-permute-start.34
  609.6 5.7 collective-permute-done.35
  622.1 4.3 collective-permute-done.37
  627.6 11.9 %gather_fusion.16 = f32[3072,6]{1,0:T(8,128)} fusion(f32[6,1216]{0,1:T(8,128)} %copy.188, s32[3072]{0:T(1024)S(1)} %broadcast_clamp_fusion), kind=kCustom, calls=%fused_computation.16 | custom fusion | bytes 159744 | tf_op jit(solution)/shard_map/gather | solution.py:36
  648.5 4.3 collective-permute-done.39
  655.3 11.9 %gather_fusion.17 = f32[3072,6]{1,0:T(8,128)} fusion(f32[6,1216]{0,1:T(8,128)} %copy.190, s32[3072]{0:T(1024)S(1)} %broadcast_clamp_fusion), kind=kCustom, calls=%fused_computation.17 | custom fusion | bytes 159744 | tf_op jit(solution)/shard_map/gather | solution.py:36
  676.2 4.3 collective-permute-done.41
  686.5 38.0 %collective-permute-start.42 = (f32[64,96]{1,0:T(8,128)S(1)}, f32[64,96]{1,0:T(8,128)S(1)}, u32[]{:S(2)}, u32[]{:S(2)}) collective-permute-start(f32[64,96]{1,0:T(8,128)S(1)} %get-tuple-element.63), channel_id=1, source_target_pairs={{0,1},{1,2},{2,3},{3,4},{4,5},{5,6},{6,7},{7,8},{8,9},{9,10},{10,1... | collective-permute-start | bytes 73736 | tf_op jit(solution)/shard_map/ppermute | solution.py:19
  726.5 8.7 %collective-permute-done.43 = f32[64,96]{1,0:T(8,128)S(1)} collective-permute-done((f32[64,96]{1,0:T(8,128)S(1)}, f32[64,96]{1,0:T(8,128)S(1)}, u32[]{:S(2)}, u32[]{:S(2)}) %collective-permute-start.43) | collective-permute-done | bytes 24608 | tf_op jit(solution)/shard_map/ppermute | solution.py:20
  744.9 8.2 %collective-permute-done.45 = f32[64,96]{1,0:T(8,128)S(1)} collective-permute-done((f32[64,96]{1,0:T(8,128)S(1)}, f32[64,96]{1,0:T(8,128)S(1)}, u32[]{:S(2)}, u32[]{:S(2)}) %collective-permute-start.45) | collective-permute-done | bytes 24608 | tf_op jit(solution)/shard_map/ppermute | solution.py:20
  (279 shorter events, 222.1 us)
Async XLA Ops:
  0.0 216.1 %copy-start = (f32[24,1536]{1,0:T(8,128)S(1)}, f32[24,1536]{1,0:T(8,128)}, u32[]{:S(2)}) copy-start(f32[24,1536]{1,0:T(8,128)} %param.25) | copy-start | bytes 442372
  4.9 11.6 %collective-permute-start = (f32[64,96]{1,0:T(8,128)S(1)}, f32[64,96]{1,0:T(8,128)S(1)}, u32[]{:S(2)}, u32[]{:S(2)}) collective-permute-start(f32[64,96]{1,0:T(8,128)S(1)} %get-tuple-element.97), channel_id=1, source_target_pairs={{0,1},{1,2},{2,3},{3,4},{4,5},{5,6},{6,7},{7,8},{8,9},{9,10},{10,1... | collective-permute-start | bytes 73736 | tf_op jit(solution)/shard_map/ppermute | solution.py:19
  9.8 10.7 %collective-permute-start.1 = (f32[64,96]{1,0:T(8,128)S(1)}, f32[64,96]{1,0:T(8,128)S(1)}, u32[]{:S(2)}, u32[]{:S(2)}) collective-permute-start(f32[64,96]{1,0:T(8,128)S(1)} %get-tuple-element.98), channel_id=1, source_target_pairs={{1,0},{2,1},{3,2},{4,3},{5,4},{6,5},{7,6},{8,7},{9,8},{10,9},{11,1... | collective-permute-start | bytes 73736 | tf_op jit(solution)/shard_map/ppermute | solution.py:20
  25.9 7.7 %collective-permute-start.2 = (f32[64,96]{1,0:T(8,128)S(1)}, f32[64,96]{1,0:T(8,128)S(1)}, u32[]{:S(2)}, u32[]{:S(2)}) collective-permute-start(f32[64,96]{1,0:T(8,128)S(1)} %get-tuple-element.95), channel_id=1, source_target_pairs={{0,1},{1,2},{2,3},{3,4},{4,5},{5,6},{6,7},{7,8},{8,9},{9,10},{10,1... | collective-permute-start | bytes 73736 | tf_op jit(solution)/shard_map/ppermute | solution.py:19
  31.1 10.7 %collective-permute-start.3 = (f32[64,96]{1,0:T(8,128)S(1)}, f32[64,96]{1,0:T(8,128)S(1)}, u32[]{:S(2)}, u32[]{:S(2)}) collective-permute-start(f32[64,96]{1,0:T(8,128)S(1)} %get-tuple-element.96), channel_id=1, source_target_pairs={{1,0},{2,1},{3,2},{4,3},{5,4},{6,5},{7,6},{8,7},{9,8},{10,9},{11,1... | collective-permute-start | bytes 73736 | tf_op jit(solution)/shard_map/ppermute | solution.py:20
  77.8 7.3 collective-permute-start.4
  81.8 7.7 %collective-permute-start.5 = (f32[6,96]{1,0:T(8,128)S(1)}, f32[6,96]{1,0:T(8,128)S(1)}, u32[]{:S(2)}, u32[]{:S(2)}) collective-permute-start(f32[6,96]{1,0:T(8,128)S(1)} %get-tuple-element.59), channel_id=1, source_target_pairs={{8,0},{16,8},{24,16},{32,24},{40,32},{48,40},{56,48},{64,56},{72,6... | collective-permute-start | bytes 6920 | tf_op jit(solution)/shard_map/ppermute | solution.py:28
  89.8 6.0 collective-permute-start.6
  91.7 7.7 %collective-permute-start.7 = (f32[6,96]{1,0:T(8,128)S(1)}, f32[6,96]{1,0:T(8,128)S(1)}, u32[]{:S(2)}, u32[]{:S(2)}) collective-permute-start(f32[6,96]{1,0:T(8,128)S(1)} %get-tuple-element.93), channel_id=1, source_target_pairs={{8,0},{16,8},{24,16},{32,24},{40,32},{48,40},{56,48},{64,56},{72,6... | collective-permute-start | bytes 6920 | tf_op jit(solution)/shard_map/ppermute | solution.py:20
  115.5 5.3 collective-permute-start.8
  117.4 7.7 %collective-permute-start.9 = (f32[6,96]{1,0:T(8,128)S(1)}, f32[6,96]{1,0:T(8,128)S(1)}, u32[]{:S(2)}, u32[]{:S(2)}) collective-permute-start(f32[6,96]{1,0:T(8,128)S(1)} %get-tuple-element.91), channel_id=1, source_target_pairs={{8,0},{16,8},{24,16},{32,24},{40,32},{48,40},{56,48},{64,56},{72,6... | collective-permute-start | bytes 6920 | tf_op jit(solution)/shard_map/ppermute | solution.py:20
  216.3 6.1 collective-permute-start.10
  220.5 7.6 %collective-permute-start.11 = (f32[1,24]{1,0:T(1,128)S(1)}, f32[1,24]{1,0:T(1,128)S(1)}, u32[]{:S(2)}, u32[]{:S(2)}) collective-permute-start(f32[1,24]{1,0:T(1,128)S(1)} %fusion.65), channel_id=1, source_target_pairs={{8,0},{16,8},{24,16},{32,24},{40,32},{48,40},{56,48},{64,56},{72,6... | collective-permute-start | bytes 296 | tf_op jit(solution)/shard_map/ppermute | solution.py:20
  229.6 5.3 collective-permute-start.12
  231.5 7.7 %collective-permute-start.13 = (f32[6,96]{1,0:T(8,128)S(1)}, f32[6,96]{1,0:T(8,128)S(1)}, u32[]{:S(2)}, u32[]{:S(2)}) collective-permute-start(f32[6,96]{1,0:T(8,128)S(1)} %get-tuple-element.89), channel_id=1, source_target_pairs={{8,0},{16,8},{24,16},{32,24},{40,32},{48,40},{56,48},{64,56},{72,6... | collective-permute-start | bytes 6920 | tf_op jit(solution)/shard_map/ppermute | solution.py:20
  255.9 93.1 %copy-start.13 = (s32[1024]{0:T(1024)S(1)}, s32[1024]{0:T(1024)}, u32[]{:S(2)}) copy-start(s32[1024]{0:T(1024)} %pad_clamp_fusion.1) | copy-start | bytes 12292
  256.0 5.3 collective-permute-start.14
  257.9 7.7 %collective-permute-start.15 = (f32[6,96]{1,0:T(8,128)S(1)}, f32[6,96]{1,0:T(8,128)S(1)}, u32[]{:S(2)}, u32[]{:S(2)}) collective-permute-start(f32[6,96]{1,0:T(8,128)S(1)} %get-tuple-element.87), channel_id=1, source_target_pairs={{8,0},{16,8},{24,16},{32,24},{40,32},{48,40},{56,48},{64,56},{72,6... | collective-permute-start | bytes 6920 | tf_op jit(solution)/shard_map/ppermute | solution.py:20
  283.8 5.3 collective-permute-start.16
  285.7 7.7 %collective-permute-start.17 = (f32[6,96]{1,0:T(8,128)S(1)}, f32[6,96]{1,0:T(8,128)S(1)}, u32[]{:S(2)}, u32[]{:S(2)}) collective-permute-start(f32[6,96]{1,0:T(8,128)S(1)} %get-tuple-element.85), channel_id=1, source_target_pairs={{8,0},{16,8},{24,16},{32,24},{40,32},{48,40},{56,48},{64,56},{72,6... | collective-permute-start | bytes 6920 | tf_op jit(solution)/shard_map/ppermute | solution.py:20
  299.4 40.1 %collective-permute-start.18 = (f32[64,96]{1,0:T(8,128)S(1)}, f32[64,96]{1,0:T(8,128)S(1)}, u32[]{:S(2)}, u32[]{:S(2)}) collective-permute-start(f32[64,96]{1,0:T(8,128)S(1)} %get-tuple-element.83), channel_id=1, source_target_pairs={{0,1},{1,2},{2,3},{3,4},{4,5},{5,6},{6,7},{7,8},{8,9},{9,10},{10,1... | collective-permute-start | bytes 73736 | tf_op jit(solution)/shard_map/ppermute | solution.py:19
  337.4 10.7 %collective-permute-start.19 = (f32[64,96]{1,0:T(8,128)S(1)}, f32[64,96]{1,0:T(8,128)S(1)}, u32[]{:S(2)}, u32[]{:S(2)}) collective-permute-start(f32[64,96]{1,0:T(8,128)S(1)} %get-tuple-element.84), channel_id=1, source_target_pairs={{1,0},{2,1},{3,2},{4,3},{5,4},{6,5},{7,6},{8,7},{9,8},{10,9},{11,1... | collective-permute-start | bytes 73736 | tf_op jit(solution)/shard_map/ppermute | solution.py:20
  353.4 4.3 collective-permute-start.20
  355.4 10.7 %collective-permute-start.21 = (f32[64,96]{1,0:T(8,128)S(1)}, f32[64,96]{1,0:T(8,128)S(1)}, u32[]{:S(2)}, u32[]{:S(2)}) collective-permute-start(f32[64,96]{1,0:T(8,128)S(1)} %get-tuple-element.82), channel_id=1, source_target_pairs={{1,0},{2,1},{3,2},{4,3},{5,4},{6,5},{7,6},{8,7},{9,8},{10,9},{11,1... | collective-permute-start | bytes 73736 | tf_op jit(solution)/shard_map/ppermute | solution.py:20
  371.4 4.3 collective-permute-start.22
  373.3 10.7 %collective-permute-start.23 = (f32[64,96]{1,0:T(8,128)S(1)}, f32[64,96]{1,0:T(8,128)S(1)}, u32[]{:S(2)}, u32[]{:S(2)}) collective-permute-start(f32[64,96]{1,0:T(8,128)S(1)} %get-tuple-element.80), channel_id=1, source_target_pairs={{1,0},{2,1},{3,2},{4,3},{5,4},{6,5},{7,6},{8,7},{9,8},{10,9},{11,1... | collective-permute-start | bytes 73736 | tf_op jit(solution)/shard_map/ppermute | solution.py:20
  392.4 4.3 collective-permute-start.24
  394.3 10.7 %collective-permute-start.25 = (f32[64,96]{1,0:T(8,128)S(1)}, f32[64,96]{1,0:T(8,128)S(1)}, u32[]{:S(2)}, u32[]{:S(2)}) collective-permute-start(f32[64,96]{1,0:T(8,128)S(1)} %get-tuple-element.78), channel_id=1, source_target_pairs={{1,0},{2,1},{3,2},{4,3},{5,4},{6,5},{7,6},{8,7},{9,8},{10,9},{11,1... | collective-permute-start | bytes 73736 | tf_op jit(solution)/shard_map/ppermute | solution.py:20
  413.4 4.3 collective-permute-start.26
  415.3 10.7 %collective-permute-start.27 = (f32[64,96]{1,0:T(8,128)S(1)}, f32[64,96]{1,0:T(8,128)S(1)}, u32[]{:S(2)}, u32[]{:S(2)}) collective-permute-start(f32[64,96]{1,0:T(8,128)S(1)} %get-tuple-element.76), channel_id=1, source_target_pairs={{1,0},{2,1},{3,2},{4,3},{5,4},{6,5},{7,6},{8,7},{9,8},{10,9},{11,1... | collective-permute-start | bytes 73736 | tf_op jit(solution)/shard_map/ppermute | solution.py:20
  464.7 5.4 collective-permute-start.28
  466.6 7.7 %collective-permute-start.29 = (f32[6,96]{1,0:T(8,128)S(1)}, f32[6,96]{1,0:T(8,128)S(1)}, u32[]{:S(2)}, u32[]{:S(2)}) collective-permute-start(f32[6,96]{1,0:T(8,128)S(1)} %get-tuple-element.57), channel_id=1, source_target_pairs={{8,0},{16,8},{24,16},{32,24},{40,32},{48,40},{56,48},{64,56},{72,6... | collective-permute-start | bytes 6920 | tf_op jit(solution)/shard_map/ppermute | solution.py:28
  474.6 5.3 collective-permute-start.30
  476.6 7.7 %collective-permute-start.31 = (f32[6,96]{1,0:T(8,128)S(1)}, f32[6,96]{1,0:T(8,128)S(1)}, u32[]{:S(2)}, u32[]{:S(2)}) collective-permute-start(f32[6,96]{1,0:T(8,128)S(1)} %get-tuple-element.73), channel_id=1, source_target_pairs={{8,0},{16,8},{24,16},{32,24},{40,32},{48,40},{56,48},{64,56},{72,6... | collective-permute-start | bytes 6920 | tf_op jit(solution)/shard_map/ppermute | solution.py:20
  501.0 5.3 collective-permute-start.32
  502.9 7.7 %collective-permute-start.33 = (f32[6,96]{1,0:T(8,128)S(1)}, f32[6,96]{1,0:T(8,128)S(1)}, u32[]{:S(2)}, u32[]{:S(2)}) collective-permute-start(f32[6,96]{1,0:T(8,128)S(1)} %get-tuple-element.71), channel_id=1, source_target_pairs={{8,0},{16,8},{24,16},{32,24},{40,32},{48,40},{56,48},{64,56},{72,6... | collective-permute-start | bytes 6920 | tf_op jit(solution)/shard_map/ppermute | solution.py:20
  603.5 6.1 collective-permute-start.34
  607.7 7.6 %collective-permute-start.35 = (f32[1,24]{1,0:T(1,128)S(1)}, f32[1,24]{1,0:T(1,128)S(1)}, u32[]{:S(2)}, u32[]{:S(2)}) collective-permute-start(f32[1,24]{1,0:T(1,128)S(1)} %fusion.66), channel_id=1, source_target_pairs={{8,0},{16,8},{24,16},{32,24},{40,32},{48,40},{56,48},{64,56},{72,6... | collective-permute-start | bytes 296 | tf_op jit(solution)/shard_map/ppermute | solution.py:20
  616.8 5.3 collective-permute-start.36
  618.7 7.7 %collective-permute-start.37 = (f32[6,96]{1,0:T(8,128)S(1)}, f32[6,96]{1,0:T(8,128)S(1)}, u32[]{:S(2)}, u32[]{:S(2)}) collective-permute-start(f32[6,96]{1,0:T(8,128)S(1)} %get-tuple-element.69), channel_id=1, source_target_pairs={{8,0},{16,8},{24,16},{32,24},{40,32},{48,40},{56,48},{64,56},{72,6... | collective-permute-start | bytes 6920 | tf_op jit(solution)/shard_map/ppermute | solution.py:20
  643.2 5.3 collective-permute-start.38
  645.1 7.7 %collective-permute-start.39 = (f32[6,96]{1,0:T(8,128)S(1)}, f32[6,96]{1,0:T(8,128)S(1)}, u32[]{:S(2)}, u32[]{:S(2)}) collective-permute-start(f32[6,96]{1,0:T(8,128)S(1)} %get-tuple-element.67), channel_id=1, source_target_pairs={{8,0},{16,8},{24,16},{32,24},{40,32},{48,40},{56,48},{64,56},{72,6... | collective-permute-start | bytes 6920 | tf_op jit(solution)/shard_map/ppermute | solution.py:20
  670.9 5.3 collective-permute-start.40
  672.9 7.7 %collective-permute-start.41 = (f32[6,96]{1,0:T(8,128)S(1)}, f32[6,96]{1,0:T(8,128)S(1)}, u32[]{:S(2)}, u32[]{:S(2)}) collective-permute-start(f32[6,96]{1,0:T(8,128)S(1)} %get-tuple-element.65), channel_id=1, source_target_pairs={{8,0},{16,8},{24,16},{32,24},{40,32},{48,40},{56,48},{64,56},{72,6... | collective-permute-start | bytes 6920 | tf_op jit(solution)/shard_map/ppermute | solution.py:20
  686.5 40.0 %collective-permute-start.42 = (f32[64,96]{1,0:T(8,128)S(1)}, f32[64,96]{1,0:T(8,128)S(1)}, u32[]{:S(2)}, u32[]{:S(2)}) collective-permute-start(f32[64,96]{1,0:T(8,128)S(1)} %get-tuple-element.63), channel_id=1, source_target_pairs={{0,1},{1,2},{2,3},{3,4},{4,5},{5,6},{6,7},{7,8},{8,9},{9,10},{10,1... | collective-permute-start | bytes 73736 | tf_op jit(solution)/shard_map/ppermute | solution.py:19
  724.6 10.7 %collective-permute-start.43 = (f32[64,96]{1,0:T(8,128)S(1)}, f32[64,96]{1,0:T(8,128)S(1)}, u32[]{:S(2)}, u32[]{:S(2)}) collective-permute-start(f32[64,96]{1,0:T(8,128)S(1)} %get-tuple-element.64), channel_id=1, source_target_pairs={{1,0},{2,1},{3,2},{4,3},{5,4},{6,5},{7,6},{8,7},{9,8},{10,9},{11,1... | collective-permute-start | bytes 73736 | tf_op jit(solution)/shard_map/ppermute | solution.py:20
  740.5 4.3 collective-permute-start.44
  742.5 10.7 %collective-permute-start.45 = (f32[64,96]{1,0:T(8,128)S(1)}, f32[64,96]{1,0:T(8,128)S(1)}, u32[]{:S(2)}, u32[]{:S(2)}) collective-permute-start(f32[64,96]{1,0:T(8,128)S(1)} %get-tuple-element.62), channel_id=1, source_target_pairs={{1,0},{2,1},{3,2},{4,3},{5,4},{6,5},{7,6},{8,7},{9,8},{10,9},{11,1... | collective-permute-start | bytes 73736 | tf_op jit(solution)/shard_map/ppermute | solution.py:20
  (15 other events, 257.6 us)
where the time goes:
time: 763 us; the launch traced here: 759 us
  local copies, waits for them, and re-layouts  195 us (26%)
  blocking collectives  192 us (25%)
  starting transfers between devices  191 us (25%)
  waiting for transfers between devices  131 us (17%)
  other arithmetic  49.2 us (6%)
    all_gather x2, blocking collectives, shards(): every = lax.all_gather(parts[None], 'slab', axis=0, tiled=True)  144 us
    ppermute x21, waiting for transfers between devices, padded(): after = lax.ppermute(leading, axis, down)  124 us
    ppermute x21, starting transfers between devices, padded(): before = lax.ppermute(last, axis, up)  123 us
    gather x17, local copies, waits for them, and re-layouts, apply_local(): picked = jnp.swapaxes(extended[:, local_cols], 0, 1)  115 us
    ppermute x21, starting transfers between devices, padded(): after = lax.ppermute(leading, axis, down)  57.4 us
    psum x2, blocking collectives, shards(): partial_sum = lax.psum(partial_sum, 'sec')  48.3 us
    transpose x17, local copies, waits for them, and re-layouts, apply_local(): picked = jnp.swapaxes(extended[:, local_cols], 0, 1)  30.7 us
    concatenate x29, local copies, waits for them, and re-layouts, padded(): array = jnp.concatenate([before, array, after], axis=dim)  25 us
  transfers between devices with their start and end apart: 46, of which 23 were waited for; matrix products, arithmetic and copies ran while one was open for 1% of the time, Pallas kernels for 0%

commit v1 on v0

--- a/solution.py
+++ b/solution.py
@@ -100,7 +100,9 @@
         coarse_res = coarse_rhs - coarse_apply(coarse_sol)
         parts = jnp.sum(section_prolong * coarse_res[None, :, None, :], axis=(1, 3))
         width = parts.shape[1]
-        every = lax.all_gather(parts[None], "slab", axis=0, tiled=True)
+        part = parts[None]
+        outgoing = jnp.stack([part] * lax.axis_size("slab"))
+        every = jnp.concatenate(lax.all_to_all(outgoing, "slab", 0, 0), axis=0)
         zero = jnp.zeros((1, width), jnp.float32)
         total = (
             every[:, 1]

time: 763 us -> 615 us (0.81)
  blocking collectives: 192 us -> 92.6 us
  starting transfers between devices: 191 us -> 142 us
    all_gather x2 -> x0, blocking collectives: 144 us -> none  [shards(): every = lax.all_gather(parts[None], 'slab', axis=0, tiled=True)]
    ppermute x21, starting transfers between devices: 123 us -> 73.6 us  [padded(): before = lax.ppermute(last, axis, up)]
    all_to_all x0 -> x2, blocking collectives: none -> 44.3 us  [shards(): every = jnp.concatenate(lax.all_to_all(outgoing, 'slab', 0, 0), axis=0)]
  transfers between devices with their start and end apart: 46 -> 46, of which waited for: 23 -> 23; matrix products, arithmetic and copies ran while one was open for 1% -> 2% of each run, Pallas kernels for 0% -> 0%
where the time goes in v1:
time: 615 us; the launch traced here: 611 us
  local copies, waits for them, and re-layouts  195 us (32%)
  starting transfers between devices  142 us (23%)
  waiting for transfers between devices  131 us (21%)
  blocking collectives  92.6 us (15%)
  other arithmetic  49.8 us (8%)
    ppermute x21, waiting for transfers between devices, padded(): after = lax.ppermute(leading, axis, down)  124 us
    gather x17, local copies, waits for them, and re-layouts, apply_local(): picked = jnp.swapaxes(extended[:, local_cols], 0, 1)  115 us
    ppermute x21, starting transfers between devices, padded(): before = lax.ppermute(last, axis, up)  73.6 us
    ppermute x21, starting transfers between devices, padded(): after = lax.ppermute(leading, axis, down)  57.6 us
    psum x2, blocking collectives, shards(): partial_sum = lax.psum(partial_sum, 'sec')  48.3 us
    all_to_all x2, blocking collectives, shards(): every = jnp.concatenate(lax.all_to_all(outgoing, 'slab', 0, 0), axis=0)  44.3 us
    transpose x17, local copies, waits for them, and re-layouts, apply_local(): picked = jnp.swapaxes(extended[:, local_cols], 0, 1)  30.7 us
    concatenate x29, local copies, waits for them, and re-layouts, padded(): array = jnp.concatenate([before, array, after], axis=dim)  25 us
  transfers between devices with their start and end apart: 46, of which 23 were waited for; matrix products, arithmetic and copies ran while one was open for 2% of the time, Pallas kernels for 0%

profile of v1, /device:TPU:127, one launch (start us, length us, event | category | flops | bytes accessed | tf_op | source)
XLA Modules:
  0.0 611.1 jit_solution(4412161457592051906)
XLA Ops:
  4.9 4.9 collective-permute-start
  16.5 3.9 collective-permute-done.1
  25.9 5.1 collective-permute-start.2
  33.6 8.1 %collective-permute-done.3 = f32[64,96]{1,0:T(8,128)S(1)} collective-permute-done((f32[64,96]{1,0:T(8,128)S(1)}, f32[64,96]{1,0:T(8,128)S(1)}, u32[]{:S(2)}, u32[]{:S(2)}) %collective-permute-start.3) | collective-permute-done | bytes 24608 | tf_op jit(solution)/shard_map/ppermute | solution.py:20
  53.9 23.9 %psum.14 = f32[6,1216]{1,0:T(8,128)S(1)} all-reduce(f32[6,1216]{1,0:T(8,128)S(1)} %copy.191), channel_id=1, replica_groups=mesh['slab'=64,'sec'=8] {'sec'}, use_global_device_ids=true, to_apply=%region_4.5 | all-reduce | flops 7296 | bytes 58368 | tf_op jit(solution)/shard_map/psum | solution.py:94
  86.0 3.4 collective-permute-done.5
  91.7 3.4 collective-permute-start.7
  95.8 3.6 collective-permute-done.7
  100.5 11.9 %gather_fusion.4 = f32[3072,6]{1,0:T(8,128)} fusion(f32[6,1216]{0,1:T(8,128)} %copy.192, s32[3072]{0:T(1024)S(1)} %broadcast_clamp_fusion), kind=kCustom, calls=%fused_computation.4 | custom fusion | bytes 159744 | tf_op jit(solution)/shard_map/gather | solution.py:36
  117.4 3.4 collective-permute-start.9
  120.8 4.3 collective-permute-done.9
  126.3 11.9 %gather_fusion.5 = f32[3072,6]{1,0:T(8,128)} fusion(f32[6,1216]{0,1:T(8,128)} %copy.194, s32[3072]{0:T(1024)S(1)} %broadcast_clamp_fusion), kind=kCustom, calls=%fused_computation.5 | custom fusion | bytes 159744 | tf_op jit(solution)/shard_map/gather | solution.py:36
  142.7 24.2 %all_to_all.10 = f32[64,1,3,24]{3,1,2,0:T(1,128)S(1)} all-to-all(f32[64,1,3,24]{3,1,2,0:T(1,128)S(1)} %stack.6), channel_id=1, replica_groups=mesh['slab'=64,'sec'=8] {'slab'}, dimensions={0} | all-to-all | bytes 36864 | tf_op jit(solution)/shard_map/all_to_all | solution.py:105
  169.5 4.0 collective-permute-start.10
  175.5 5.7 collective-permute-done.11
  188.0 4.3 collective-permute-done.13
  193.5 11.9 %gather_fusion.6 = f32[3072,6]{1,0:T(8,128)} fusion(f32[6,1216]{0,1:T(8,128)} %copy.198, s32[3072]{0:T(1024)S(1)} %broadcast_clamp_fusion), kind=kCustom, calls=%fused_computation.6 | custom fusion | bytes 159744 | tf_op jit(solution)/shard_map/gather | solution.py:36
  211.0 3.4 collective-permute-start.15
  214.4 4.3 collective-permute-done.15
  221.2 11.9 %gather_fusion.7 = f32[3072,6]{1,0:T(8,128)} fusion(f32[6,1216]{0,1:T(8,128)} %copy.200, s32[3072]{0:T(1024)S(1)} %broadcast_clamp_fusion), kind=kCustom, calls=%fused_computation.7 | custom fusion | bytes 159744 | tf_op jit(solution)/shard_map/gather | solution.py:36
  238.8 3.5 collective-permute-start.17
  242.3 4.1 collective-permute-done.17
  252.5 13.5 %collective-permute-start.18 = (f32[64,96]{1,0:T(8,128)S(1)}, f32[64,96]{1,0:T(8,128)S(1)}, u32[]{:S(2)}, u32[]{:S(2)}) collective-permute-start(f32[64,96]{1,0:T(8,128)S(1)} %get-tuple-element.83), channel_id=1, source_target_pairs={{0,1},{1,2},{2,3},{3,4},{4,5},{5,6},{6,7},{7,8},{8,9},{9,10},{10,1... | collective-permute-start | bytes 73736 | tf_op jit(solution)/shard_map/ppermute | solution.py:19
  267.9 8.7 %collective-permute-done.19 = f32[64,96]{1,0:T(8,128)S(1)} collective-permute-done((f32[64,96]{1,0:T(8,128)S(1)}, f32[64,96]{1,0:T(8,128)S(1)}, u32[]{:S(2)}, u32[]{:S(2)}) %collective-permute-start.19) | collective-permute-done | bytes 24608 | tf_op jit(solution)/shard_map/ppermute | solution.py:20
  286.3 8.2 %collective-permute-done.21 = f32[64,96]{1,0:T(8,128)S(1)} collective-permute-done((f32[64,96]{1,0:T(8,128)S(1)}, f32[64,96]{1,0:T(8,128)S(1)}, u32[]{:S(2)}, u32[]{:S(2)}) %collective-permute-start.21) | collective-permute-done | bytes 24608 | tf_op jit(solution)/shard_map/ppermute | solution.py:20
  304.3 8.2 %collective-permute-done.23 = f32[64,96]{1,0:T(8,128)S(1)} collective-permute-done((f32[64,96]{1,0:T(8,128)S(1)}, f32[64,96]{1,0:T(8,128)S(1)}, u32[]{:S(2)}, u32[]{:S(2)}) %collective-permute-start.23) | collective-permute-done | bytes 24608 | tf_op jit(solution)/shard_map/ppermute | solution.py:20
  325.2 8.2 %collective-permute-done.25 = f32[64,96]{1,0:T(8,128)S(1)} collective-permute-done((f32[64,96]{1,0:T(8,128)S(1)}, f32[64,96]{1,0:T(8,128)S(1)}, u32[]{:S(2)}, u32[]{:S(2)}) %collective-permute-start.25) | collective-permute-done | bytes 24608 | tf_op jit(solution)/shard_map/ppermute | solution.py:20
  346.2 8.2 %collective-permute-done.27 = f32[64,96]{1,0:T(8,128)S(1)} collective-permute-done((f32[64,96]{1,0:T(8,128)S(1)}, f32[64,96]{1,0:T(8,128)S(1)}, u32[]{:S(2)}, u32[]{:S(2)}) %collective-permute-start.27) | collective-permute-done | bytes 24608 | tf_op jit(solution)/shard_map/ppermute | solution.py:20
  368.7 24.5 %psum.15 = f32[6,1216]{1,0:T(8,128)S(1)} all-reduce(f32[6,1216]{1,0:T(8,128)} %copy.215), channel_id=1, replica_groups=mesh['slab'=64,'sec'=8] {'sec'}, use_global_device_ids=true, to_apply=%region_20.21 | all-reduce | flops 7296 | bytes 58368 | tf_op jit(solution)/shard_map/psum | solution.py:94
  399.4 3.4 collective-permute-done.29
  408.5 4.3 collective-permute-done.31
  413.9 11.9 %gather_fusion.14 = f32[3072,6]{1,0:T(8,128)} fusion(f32[6,1216]{0,1:T(8,128)} %copy.216, s32[3072]{0:T(1024)S(1)} %broadcast_clamp_fusion), kind=kCustom, calls=%fused_computation.14 | custom fusion | bytes 159744 | tf_op jit(solution)/shard_map/gather | solution.py:36
  431.5 3.6 collective-permute-start.33
  435.1 4.1 collective-permute-done.33
  440.3 11.9 %gather_fusion.15 = f32[3072,6]{1,0:T(8,128)} fusion(f32[6,1216]{0,1:T(8,128)} %copy.218, s32[3072]{0:T(1024)S(1)} %broadcast_clamp_fusion), kind=kCustom, calls=%fused_computation.15 | custom fusion | bytes 159744 | tf_op jit(solution)/shard_map/gather | solution.py:36
  457.4 20.2 %all_to_all.11 = f32[64,1,3,24]{3,1,2,0:T(1,128)} all-to-all(f32[64,1,3,24]{3,1,2,0:T(1,128)S(1)} %stack.7), channel_id=1, replica_groups=mesh['slab'=64,'sec'=8] {'slab'}, dimensions={0} | all-to-all | bytes 36864 | tf_op jit(solution)/shard_map/all_to_all | solution.py:105
  480.3 4.0 collective-permute-start.34
  486.3 5.7 collective-permute-done.35
  495.4 3.4 collective-permute-start.37
  498.8 4.3 collective-permute-done.37
  504.3 11.9 %gather_fusion.16 = f32[3072,6]{1,0:T(8,128)} fusion(f32[6,1216]{0,1:T(8,128)} %copy.222, s32[3072]{0:T(1024)S(1)} %broadcast_clamp_fusion), kind=kCustom, calls=%fused_computation.16 | custom fusion | bytes 159744 | tf_op jit(solution)/shard_map/gather | solution.py:36
  521.8 3.4 collective-permute-start.39
  525.2 4.3 collective-permute-done.39
  532.0 11.9 %gather_fusion.17 = f32[3072,6]{1,0:T(8,128)} fusion(f32[6,1216]{0,1:T(8,128)} %copy.224, s32[3072]{0:T(1024)S(1)} %broadcast_clamp_fusion), kind=kCustom, calls=%fused_computation.17 | custom fusion | bytes 159744 | tf_op jit(solution)/shard_map/gather | solution.py:36
  552.9 4.3 collective-permute-done.41
  563.2 13.5 %collective-permute-start.42 = (f32[64,96]{1,0:T(8,128)S(1)}, f32[64,96]{1,0:T(8,128)S(1)}, u32[]{:S(2)}, u32[]{:S(2)}) collective-permute-start(f32[64,96]{1,0:T(8,128)S(1)} %get-tuple-element.63), channel_id=1, source_target_pairs={{0,1},{1,2},{2,3},{3,4},{4,5},{5,6},{6,7},{7,8},{8,9},{9,10},{10,1... | collective-permute-start | bytes 73736 | tf_op jit(solution)/shard_map/ppermute | solution.py:19
  578.6 8.7 %collective-permute-done.43 = f32[64,96]{1,0:T(8,128)S(1)} collective-permute-done((f32[64,96]{1,0:T(8,128)S(1)}, f32[64,96]{1,0:T(8,128)S(1)}, u32[]{:S(2)}, u32[]{:S(2)}) %collective-permute-start.43) | collective-permute-done | bytes 24608 | tf_op jit(solution)/shard_map/ppermute | solution.py:20
  597.0 8.2 %collective-permute-done.45 = f32[64,96]{1,0:T(8,128)S(1)} collective-permute-done((f32[64,96]{1,0:T(8,128)S(1)}, f32[64,96]{1,0:T(8,128)S(1)}, u32[]{:S(2)}, u32[]{:S(2)}) %collective-permute-start.45) | collective-permute-done | bytes 24608 | tf_op jit(solution)/shard_map/ppermute | solution.py:20
  (275 shorter events, 222.7 us)
Async XLA Ops:
  0.0 169.3 %copy-start = (f32[24,1536]{1,0:T(8,128)S(1)}, f32[24,1536]{1,0:T(8,128)}, u32[]{:S(2)}) copy-start(f32[24,1536]{1,0:T(8,128)} %param.25) | copy-start | bytes 442372
  4.9 11.6 %collective-permute-start = (f32[64,96]{1,0:T(8,128)S(1)}, f32[64,96]{1,0:T(8,128)S(1)}, u32[]{:S(2)}, u32[]{:S(2)}) collective-permute-start(f32[64,96]{1,0:T(8,128)S(1)} %get-tuple-element.97), channel_id=1, source_target_pairs={{0,1},{1,2},{2,3},{3,4},{4,5},{5,6},{6,7},{7,8},{8,9},{9,10},{10,1... | collective-permute-start | bytes 73736 | tf_op jit(solution)/shard_map/ppermute | solution.py:19
  9.8 10.7 %collective-permute-start.1 = (f32[64,96]{1,0:T(8,128)S(1)}, f32[64,96]{1,0:T(8,128)S(1)}, u32[]{:S(2)}, u32[]{:S(2)}) collective-permute-start(f32[64,96]{1,0:T(8,128)S(1)} %get-tuple-element.98), channel_id=1, source_target_pairs={{1,0},{2,1},{3,2},{4,3},{5,4},{6,5},{7,6},{8,7},{9,8},{10,9},{11,1... | collective-permute-start | bytes 73736 | tf_op jit(solution)/shard_map/ppermute | solution.py:20
  25.9 7.7 %collective-permute-start.2 = (f32[64,96]{1,0:T(8,128)S(1)}, f32[64,96]{1,0:T(8,128)S(1)}, u32[]{:S(2)}, u32[]{:S(2)}) collective-permute-start(f32[64,96]{1,0:T(8,128)S(1)} %get-tuple-element.95), channel_id=1, source_target_pairs={{0,1},{1,2},{2,3},{3,4},{4,5},{5,6},{6,7},{7,8},{8,9},{9,10},{10,1... | collective-permute-start | bytes 73736 | tf_op jit(solution)/shard_map/ppermute | solution.py:19
  31.1 10.7 %collective-permute-start.3 = (f32[64,96]{1,0:T(8,128)S(1)}, f32[64,96]{1,0:T(8,128)S(1)}, u32[]{:S(2)}, u32[]{:S(2)}) collective-permute-start(f32[64,96]{1,0:T(8,128)S(1)} %get-tuple-element.96), channel_id=1, source_target_pairs={{1,0},{2,1},{3,2},{4,3},{5,4},{6,5},{7,6},{8,7},{9,8},{10,9},{11,1... | collective-permute-start | bytes 73736 | tf_op jit(solution)/shard_map/ppermute | solution.py:20
  77.8 7.3 %collective-permute-start.4 = (f32[6,96]{1,0:T(8,128)S(1)}, f32[6,96]{1,0:T(8,128)S(1)}, u32[]{:S(2)}, u32[]{:S(2)}) collective-permute-start(f32[6,96]{1,0:T(8,128)S(1)} %get-tuple-element.56), channel_id=1, source_target_pairs={{0,8},{8,16},{16,24},{24,32},{32,40},{40,48},{48,56},{56,64},{64,7... | collective-permute-start | bytes 6920 | tf_op jit(solution)/shard_map/ppermute | solution.py:28
  81.8 7.7 %collective-permute-start.5 = (f32[6,96]{1,0:T(8,128)S(1)}, f32[6,96]{1,0:T(8,128)S(1)}, u32[]{:S(2)}, u32[]{:S(2)}) collective-permute-start(f32[6,96]{1,0:T(8,128)S(1)} %get-tuple-element.55), channel_id=1, source_target_pairs={{8,0},{16,8},{24,16},{32,24},{40,32},{48,40},{56,48},{64,56},{72,6... | collective-permute-start | bytes 6920 | tf_op jit(solution)/shard_map/ppermute | solution.py:28
  89.8 6.0 collective-permute-start.6
  91.7 7.7 %collective-permute-start.7 = (f32[6,96]{1,0:T(8,128)S(1)}, f32[6,96]{1,0:T(8,128)S(1)}, u32[]{:S(2)}, u32[]{:S(2)}) collective-permute-start(f32[6,96]{1,0:T(8,128)S(1)} %get-tuple-element.93), channel_id=1, source_target_pairs={{8,0},{16,8},{24,16},{32,24},{40,32},{48,40},{56,48},{64,56},{72,6... | collective-permute-start | bytes 6920 | tf_op jit(solution)/shard_map/ppermute | solution.py:20
  115.5 5.3 collective-permute-start.8
  117.4 7.7 %collective-permute-start.9 = (f32[6,96]{1,0:T(8,128)S(1)}, f32[6,96]{1,0:T(8,128)S(1)}, u32[]{:S(2)}, u32[]{:S(2)}) collective-permute-start(f32[6,96]{1,0:T(8,128)S(1)} %get-tuple-element.91), channel_id=1, source_target_pairs={{8,0},{16,8},{24,16},{32,24},{40,32},{48,40},{56,48},{64,56},{72,6... | collective-permute-start | bytes 6920 | tf_op jit(solution)/shard_map/ppermute | solution.py:20
  169.5 6.0 collective-permute-start.10
  173.5 7.6 %collective-permute-start.11 = (f32[1,24]{1,0:T(1,128)S(1)}, f32[1,24]{1,0:T(1,128)S(1)}, u32[]{:S(2)}, u32[]{:S(2)}) collective-permute-start(f32[1,24]{1,0:T(1,128)S(1)} %fusion.65), channel_id=1, source_target_pairs={{8,0},{16,8},{24,16},{32,24},{40,32},{48,40},{56,48},{64,56},{72,6... | collective-permute-start | bytes 296 | tf_op jit(solution)/shard_map/ppermute | solution.py:20
  182.7 5.3 collective-permute-start.12
  184.6 7.7 %collective-permute-start.13 = (f32[6,96]{1,0:T(8,128)S(1)}, f32[6,96]{1,0:T(8,128)S(1)}, u32[]{:S(2)}, u32[]{:S(2)}) collective-permute-start(f32[6,96]{1,0:T(8,128)S(1)} %get-tuple-element.89), channel_id=1, source_target_pairs={{8,0},{16,8},{24,16},{32,24},{40,32},{48,40},{56,48},{64,56},{72,6... | collective-permute-start | bytes 6920 | tf_op jit(solution)/shard_map/ppermute | solution.py:20
  209.0 68.5 %copy-start.13 = (s32[1024]{0:T(1024)S(1)}, s32[1024]{0:T(1024)}, u32[]{:S(2)}) copy-start(s32[1024]{0:T(1024)} %pad_clamp_fusion.1) | copy-start | bytes 12292
  209.1 5.3 collective-permute-start.14
  211.0 7.7 %collective-permute-start.15 = (f32[6,96]{1,0:T(8,128)S(1)}, f32[6,96]{1,0:T(8,128)S(1)}, u32[]{:S(2)}, u32[]{:S(2)}) collective-permute-start(f32[6,96]{1,0:T(8,128)S(1)} %get-tuple-element.87), channel_id=1, source_target_pairs={{8,0},{16,8},{24,16},{32,24},{40,32},{48,40},{56,48},{64,56},{72,6... | collective-permute-start | bytes 6920 | tf_op jit(solution)/shard_map/ppermute | solution.py:20
  236.8 5.5 collective-permute-start.16
  238.8 7.7 %collective-permute-start.17 = (f32[6,96]{1,0:T(8,128)S(1)}, f32[6,96]{1,0:T(8,128)S(1)}, u32[]{:S(2)}, u32[]{:S(2)}) collective-permute-start(f32[6,96]{1,0:T(8,128)S(1)} %get-tuple-element.85), channel_id=1, source_target_pairs={{8,0},{16,8},{24,16},{32,24},{40,32},{48,40},{56,48},{64,56},{72,6... | collective-permute-start | bytes 6920 | tf_op jit(solution)/shard_map/ppermute | solution.py:20
  252.5 15.4 %collective-permute-start.18 = (f32[64,96]{1,0:T(8,128)S(1)}, f32[64,96]{1,0:T(8,128)S(1)}, u32[]{:S(2)}, u32[]{:S(2)}) collective-permute-start(f32[64,96]{1,0:T(8,128)S(1)} %get-tuple-element.83), channel_id=1, source_target_pairs={{0,1},{1,2},{2,3},{3,4},{4,5},{5,6},{6,7},{7,8},{8,9},{9,10},{10,1... | collective-permute-start | bytes 73736 | tf_op jit(solution)/shard_map/ppermute | solution.py:19
  265.9 10.7 %collective-permute-start.19 = (f32[64,96]{1,0:T(8,128)S(1)}, f32[64,96]{1,0:T(8,128)S(1)}, u32[]{:S(2)}, u32[]{:S(2)}) collective-permute-start(f32[64,96]{1,0:T(8,128)S(1)} %get-tuple-element.84), channel_id=1, source_target_pairs={{1,0},{2,1},{3,2},{4,3},{5,4},{6,5},{7,6},{8,7},{9,8},{10,9},{11,1... | collective-permute-start | bytes 73736 | tf_op jit(solution)/shard_map/ppermute | solution.py:20
  282.0 4.3 collective-permute-start.20
  283.9 10.7 %collective-permute-start.21 = (f32[64,96]{1,0:T(8,128)S(1)}, f32[64,96]{1,0:T(8,128)S(1)}, u32[]{:S(2)}, u32[]{:S(2)}) collective-permute-start(f32[64,96]{1,0:T(8,128)S(1)} %get-tuple-element.82), channel_id=1, source_target_pairs={{1,0},{2,1},{3,2},{4,3},{5,4},{6,5},{7,6},{8,7},{9,8},{10,9},{11,1... | collective-permute-start | bytes 73736 | tf_op jit(solution)/shard_map/ppermute | solution.py:20
  299.9 4.3 collective-permute-start.22
  301.8 10.7 %collective-permute-start.23 = (f32[64,96]{1,0:T(8,128)S(1)}, f32[64,96]{1,0:T(8,128)S(1)}, u32[]{:S(2)}, u32[]{:S(2)}) collective-permute-start(f32[64,96]{1,0:T(8,128)S(1)} %get-tuple-element.80), channel_id=1, source_target_pairs={{1,0},{2,1},{3,2},{4,3},{5,4},{6,5},{7,6},{8,7},{9,8},{10,9},{11,1... | collective-permute-start | bytes 73736 | tf_op jit(solution)/shard_map/ppermute | solution.py:20
  320.9 4.3 collective-permute-start.24
  322.8 10.7 %collective-permute-start.25 = (f32[64,96]{1,0:T(8,128)S(1)}, f32[64,96]{1,0:T(8,128)S(1)}, u32[]{:S(2)}, u32[]{:S(2)}) collective-permute-start(f32[64,96]{1,0:T(8,128)S(1)} %get-tuple-element.78), channel_id=1, source_target_pairs={{1,0},{2,1},{3,2},{4,3},{5,4},{6,5},{7,6},{8,7},{9,8},{10,9},{11,1... | collective-permute-start | bytes 73736 | tf_op jit(solution)/shard_map/ppermute | solution.py:20
  341.9 4.3 collective-permute-start.26
  343.8 10.7 %collective-permute-start.27 = (f32[64,96]{1,0:T(8,128)S(1)}, f32[64,96]{1,0:T(8,128)S(1)}, u32[]{:S(2)}, u32[]{:S(2)}) collective-permute-start(f32[64,96]{1,0:T(8,128)S(1)} %get-tuple-element.76), channel_id=1, source_target_pairs={{1,0},{2,1},{3,2},{4,3},{5,4},{6,5},{7,6},{8,7},{9,8},{10,9},{11,1... | collective-permute-start | bytes 73736 | tf_op jit(solution)/shard_map/ppermute | solution.py:20
  393.2 5.4 collective-permute-start.28
  395.2 7.7 %collective-permute-start.29 = (f32[6,96]{1,0:T(8,128)S(1)}, f32[6,96]{1,0:T(8,128)S(1)}, u32[]{:S(2)}, u32[]{:S(2)}) collective-permute-start(f32[6,96]{1,0:T(8,128)S(1)} %get-tuple-element.53), channel_id=1, source_target_pairs={{8,0},{16,8},{24,16},{32,24},{40,32},{48,40},{56,48},{64,56},{72,6... | collective-permute-start | bytes 6920 | tf_op jit(solution)/shard_map/ppermute | solution.py:28
  403.2 5.3 collective-permute-start.30
  405.1 7.7 %collective-permute-start.31 = (f32[6,96]{1,0:T(8,128)S(1)}, f32[6,96]{1,0:T(8,128)S(1)}, u32[]{:S(2)}, u32[]{:S(2)}) collective-permute-start(f32[6,96]{1,0:T(8,128)S(1)} %get-tuple-element.73), channel_id=1, source_target_pairs={{8,0},{16,8},{24,16},{32,24},{40,32},{48,40},{56,48},{64,56},{72,6... | collective-permute-start | bytes 6920 | tf_op jit(solution)/shard_map/ppermute | solution.py:20
  429.6 5.5 collective-permute-start.32
  431.5 7.7 %collective-permute-start.33 = (f32[6,96]{1,0:T(8,128)S(1)}, f32[6,96]{1,0:T(8,128)S(1)}, u32[]{:S(2)}, u32[]{:S(2)}) collective-permute-start(f32[6,96]{1,0:T(8,128)S(1)} %get-tuple-element.71), channel_id=1, source_target_pairs={{8,0},{16,8},{24,16},{32,24},{40,32},{48,40},{56,48},{64,56},{72,6... | collective-permute-start | bytes 6920 | tf_op jit(solution)/shard_map/ppermute | solution.py:20
  480.3 6.0 collective-permute-start.34
  484.4 7.6 %collective-permute-start.35 = (f32[1,24]{1,0:T(1,128)S(1)}, f32[1,24]{1,0:T(1,128)S(1)}, u32[]{:S(2)}, u32[]{:S(2)}) collective-permute-start(f32[1,24]{1,0:T(1,128)S(1)} %fusion.66), channel_id=1, source_target_pairs={{8,0},{16,8},{24,16},{32,24},{40,32},{48,40},{56,48},{64,56},{72,6... | collective-permute-start | bytes 296 | tf_op jit(solution)/shard_map/ppermute | solution.py:20
  493.5 5.3 collective-permute-start.36
  495.4 7.7 %collective-permute-start.37 = (f32[6,96]{1,0:T(8,128)S(1)}, f32[6,96]{1,0:T(8,128)S(1)}, u32[]{:S(2)}, u32[]{:S(2)}) collective-permute-start(f32[6,96]{1,0:T(8,128)S(1)} %get-tuple-element.69), channel_id=1, source_target_pairs={{8,0},{16,8},{24,16},{32,24},{40,32},{48,40},{56,48},{64,56},{72,6... | collective-permute-start | bytes 6920 | tf_op jit(solution)/shard_map/ppermute | solution.py:20
  519.9 5.3 collective-permute-start.38
  521.8 7.7 %collective-permute-start.39 = (f32[6,96]{1,0:T(8,128)S(1)}, f32[6,96]{1,0:T(8,128)S(1)}, u32[]{:S(2)}, u32[]{:S(2)}) collective-permute-start(f32[6,96]{1,0:T(8,128)S(1)} %get-tuple-element.67), channel_id=1, source_target_pairs={{8,0},{16,8},{24,16},{32,24},{40,32},{48,40},{56,48},{64,56},{72,6... | collective-permute-start | bytes 6920 | tf_op jit(solution)/shard_map/ppermute | solution.py:20
  547.6 5.3 collective-permute-start.40
  549.6 7.7 %collective-permute-start.41 = (f32[6,96]{1,0:T(8,128)S(1)}, f32[6,96]{1,0:T(8,128)S(1)}, u32[]{:S(2)}, u32[]{:S(2)}) collective-permute-start(f32[6,96]{1,0:T(8,128)S(1)} %get-tuple-element.65), channel_id=1, source_target_pairs={{8,0},{16,8},{24,16},{32,24},{40,32},{48,40},{56,48},{64,56},{72,6... | collective-permute-start | bytes 6920 | tf_op jit(solution)/shard_map/ppermute | solution.py:20
  563.2 15.4 %collective-permute-start.42 = (f32[64,96]{1,0:T(8,128)S(1)}, f32[64,96]{1,0:T(8,128)S(1)}, u32[]{:S(2)}, u32[]{:S(2)}) collective-permute-start(f32[64,96]{1,0:T(8,128)S(1)} %get-tuple-element.63), channel_id=1, source_target_pairs={{0,1},{1,2},{2,3},{3,4},{4,5},{5,6},{6,7},{7,8},{8,9},{9,10},{10,1... | collective-permute-start | bytes 73736 | tf_op jit(solution)/shard_map/ppermute | solution.py:19
  576.7 10.7 %collective-permute-start.43 = (f32[64,96]{1,0:T(8,128)S(1)}, f32[64,96]{1,0:T(8,128)S(1)}, u32[]{:S(2)}, u32[]{:S(2)}) collective-permute-start(f32[64,96]{1,0:T(8,128)S(1)} %get-tuple-element.64), channel_id=1, source_target_pairs={{1,0},{2,1},{3,2},{4,3},{5,4},{6,5},{7,6},{8,7},{9,8},{10,9},{11,1... | collective-permute-start | bytes 73736 | tf_op jit(solution)/shard_map/ppermute | solution.py:20
  592.7 4.3 collective-permute-start.44
  594.6 10.7 %collective-permute-start.45 = (f32[64,96]{1,0:T(8,128)S(1)}, f32[64,96]{1,0:T(8,128)S(1)}, u32[]{:S(2)}, u32[]{:S(2)}) collective-permute-start(f32[64,96]{1,0:T(8,128)S(1)} %get-tuple-element.62), channel_id=1, source_target_pairs={{1,0},{2,1},{3,2},{4,3},{5,4},{6,5},{7,6},{8,7},{9,8},{10,9},{11,1... | collective-permute-start | bytes 73736 | tf_op jit(solution)/shard_map/ppermute | solution.py:20
  (15 other events, 233.2 us)
